TPU v7x, 256 devices: a whole 4x4x8 slice. The times are simulated.
256 devices in a mesh: dp: 128 (over x, y, z), head: 2 (over core).
Axes of the slice: x: 4, y: 4, z: 8, core: 2. Of those that a mesh axis runs over, the one named last changes fastest.
Arguments:
- context: bfloat16 [49152, 2048], P('dp', 'head'), may hold values from -6 to 6
- residual: bfloat16 [49152, 2048], P('dp'), may hold values from -6 to 6
- bias_out: float32 [2048], replicated, may hold values from -3 to 3
- norm_gain: float32 [2048], replicated, may hold values from 0.1 to 1.9
- out_weight: bfloat16 [2048, 2048], P('head', 'dp'), may hold values from -0.125 to 0.125
- cotangent: bfloat16 [49152, 2048], P('dp'), may hold values from -6 to 6
- counts: int32 [128], P('dp'), may hold values from 96 to 384, as said below
- slot_codes: int32 [49152], P('dp'), may hold values from 0 to 383, as said below
Outputs:
- grad_resid: bfloat16 [49152, 2048], P('dp')
- grad_ctx: bfloat16 [49152, 2048], P('dp', 'head')
- grad_wout: float32 [2048, 2048], P('head', 'dp')
Inputs may be any that keep to these rules, and one draw needn't show every extreme that they name: `counts`: one dp index has 384 live rows, every other between 96 and 192. `slot_codes`: the codes of one device are distinct; code c names decoder owner c // 3 and slot c % 3; on every device the first 3 rows go to one owner.
All inputs are finite; a program needn't handle non-finite values.
Results may differ from a plain program's by a relative error of at most 0.0049.
Values may be sent and summed in bfloat16 or wider, within the bound.
No kernel may reach another device: no remote copies, remote signals or barrier semaphores. Data moves between devices by JAX's collectives and lax.ppermute only.
A program may use at most 64 MiB of HBM per device.

v0:
```python
import jax
import jax.numpy as jnp
from jax import lax
from jax.sharding import Mesh, PartitionSpec as P

F32 = jnp.float32
BF16 = jnp.bfloat16


def norm_back(projected, residual, bias_out, norm_gain, grad_out):
    summed_in = residual.astype(F32) + projected + bias_out
    mean_in = jnp.mean(summed_in, axis=-1, keepdims=True)
    centred = summed_in - mean_in
    variance = jnp.mean(centred * centred, axis=-1, keepdims=True)
    inv_std = lax.rsqrt(variance + 1e-05)
    normed = centred * inv_std
    grad_norm = grad_out.astype(F32) * norm_gain
    first_mean = jnp.mean(grad_norm, axis=-1, keepdims=True)
    second_mean = jnp.mean(grad_norm * normed, axis=-1, keepdims=True)
    return (inv_std * (grad_norm - first_mean - normed * second_mean)).astype(BF16)


def shards(context, residual, bias_out, norm_gain, out_weight, cotangent, counts, slot_codes):
    capacity = slot_codes.shape[0]
    features = residual.shape[1]
    half = features // 2
    core = lax.axis_index("core")
    live_mask = jnp.arange(capacity) < counts[0]
    swap = [(0, 1), (1, 0)]
    mine = lax.dynamic_slice_in_dim(cotangent, core * half, half, axis=1)
    returned = lax.all_to_all(mine, ("x", "y", "z"), split_axis=0, concat_axis=0, tiled=True)
    picked = jnp.take(returned, slot_codes, axis=0)
    picked = jnp.where(live_mask[:, None], picked, jnp.zeros((), picked.dtype))
    other = lax.ppermute(picked, "core", swap)
    grad_out = jnp.where(
        core == 0,
        jnp.concatenate([picked, other], axis=1),
        jnp.concatenate([other, picked], axis=1),
    )
    weight_t = lax.all_gather(out_weight.T, "z", axis=0, tiled=True)
    weight_t = lax.all_gather(weight_t, ("x", "y"), axis=0, tiled=True)
    partial_proj = lax.dot_general(
        context, weight_t, (((1,), (1,)), ((), ())), preferred_element_type=F32
    )
    projected = partial_proj + lax.ppermute(partial_proj, "core", swap)
    grad_resid = norm_back(projected, residual, bias_out, norm_gain, grad_out)
    share = lax.dot_general(
        grad_resid, context, (((0,), (0,)), ((), ())), preferred_element_type=F32
    ).astype(BF16)
    grad_ctx = jnp.dot(grad_resid, weight_t, preferred_element_type=F32).astype(BF16)
    total = None
    for axis in ("x", "y", "z"):
        ways = lax.axis_size(axis)
        share = share.reshape(ways, -1, share.shape[-1])
        got = lax.all_to_all(share, axis, split_axis=0, concat_axis=0)
        total = jnp.sum(got.astype(F32), axis=0)
        share = total.astype(BF16)
    replicas = lax.axis_size("x") * lax.axis_size("y") * lax.axis_size("z")
    grad_wout = (total / replicas).T
    return (grad_resid, grad_ctx, grad_wout)


def solution(mesh):
    torus = Mesh(mesh.devices.reshape(4, 4, 8, 2), ("x", "y", "z", "core"))
    dp = ("x", "y", "z")
    return jax.shard_map(
        shards,
        mesh=torus,
        in_specs=(P(dp, "core"), P(dp, None), P(), P(), P("core", dp), P(dp, None), P(dp), P(dp)),
        out_specs=(P(dp, None), P(dp, "core"), P("core", dp)),
        check_vma=False,
    )
```

profile of v0, /device:TPU:2, one launch (start us, length us, event | category | flops | bytes accessed | tf_op | source)
XLA Modules:
  0.0 257.1 jit_solution(9456713248749015484)
XLA Ops:
  7.2 0.0 copy-start
  7.2 0.0 all-gather.2.cloned.1.call-start
  7.2 30.8 %all_gather.6 = bf16[128,1024]{1,0:T(8,128)(2,1)} all-gather(bf16[16,1024]{1,0:T(8,128)(2,1)} %bitcast.16), channel_id=1, replica_groups=mesh['x'=4,'y'=4,'z'=8,'core'=2] {'z'}, dimensions={0}, use_global_device_ids=true | all-gather | bytes 294912 | tf_op jit(solution)/shard_map/all_gather | solution.py:40
  38.0 0.0 all-gather.2.cloned.1.call-update
  38.0 56.2 %all-gather.2.cloned.1.call-done = bf16[2048,1024]{1,0:T(8,128)(2,1)} async-done(((bf16[128,1024]{1,0:T(8,128)(2,1)}), bf16[2048,1024]{1,0:T(8,128)(2,1)}) %all-gather.2.cloned.1.call-update) | async-done | bytes 4194320 | tf_op jit(solution)/shard_map/all_gather | solution.py:41
  94.2 5.9 %fusion.2 = f32[384,2048]{1,0:T(8,128)} fusion(bf16[384,1024]{1,0:T(8,128)(2,1)} %param.8, bf16[2048,1024]{1,0:T(8,128)(2,1)} %all-gather.2.cloned.1.call-done), kind=kOutput, calls=%fused_computation.23 | convolution fusion | flops 1610612736 | bytes 8126464 | tf_op jit(solution)/shard_map/dot_general | solution.py:42
  100.1 0.0 copy-start.3
  100.1 0.0 collective-permute-start
  100.1 0.0 copy-done
  100.1 0.1 constant_dynamic-slice_fusion
  100.2 1.3 all_to_all.17
  101.5 12.3 %all-to-all-start = ((bf16[128,3,1024]{2,1,0:T(4,128)(2,1)}), bf16[128,3,1024]{2,1,0:T(4,128)(2,1)S(1)}, u32[]{:S(2)}, u32[]{:S(2)}) async-start(bf16[128,3,1024]{2,1,0:T(4,128)(2,1)} %all_to_all.17), calls=%async_computation | async-start | bytes 2097152 | tf_op jit(solution)/shard_map/all_to_all | solution.py:31
  114.5 0.0 copy-done.3
  114.5 29.3 %all-to-all-done = bf16[128,3,1024]{2,1,0:T(4,128)(2,1)S(1)} async-done(((bf16[128,3,1024]{2,1,0:T(4,128)(2,1)}), bf16[128,3,1024]{2,1,0:T(4,128)(2,1)S(1)}, u32[]{:S(2)}, u32[]{:S(2)}) %all-to-all-start) | async-done | bytes 786464 | tf_op jit(solution)/shard_map/all_to_all | solution.py:31
  143.9 0.7 all_to_all.19
  144.5 0.0 copy-start.4
  144.6 2.1 gather_fusion
  146.6 0.2 select_select_fusion
  146.8 0.1 collective-permute-start.1
  146.9 0.0 collective-permute-done
  146.9 0.0 copy-done.4
  146.9 3.9 %fusion.1 = (f32[384]{0:T(512)S(1)}, f32[384,2048]{1,0:T(8,128)S(1)}) fusion(f32[2048]{0:T(1024)S(1)} %copy-done.4, f32[384,2048]{1,0:T(8,128)} %fusion.2, f32[384,2048]{1,0:T(8,128)} %collective-permute-done, bf16[384,2048]{1,0:T(8,128)(2,1)} %param.9), kind=kLoop, calls=%fused_computation.22 | loop fusion | flops 3931776 | bytes 11019776 | tf_op jit(solution)/shard_map/reduce_sum | solution.py:12
  150.8 0.0 copy-start.2
  150.8 0.5 multiply_reduce_fusion.1
  151.3 0.0 collective-permute-done.1
  151.3 0.2 copy-done.2
  151.5 1.0 fusion
  152.5 0.0 copy-start.5
  152.6 1.6 multiply_convert_fusion
  154.2 0.0 copy-done.5
  154.2 0.0 copy-start.1
  154.2 2.4 convolution_convert_fusion
  156.6 0.0 copy-done.1
  156.6 55.0 %all_to_all.27 = bf16[4,512,1024]{2,1,0:T(8,128)(2,1)} all-to-all(bf16[4,512,1024]{2,1,0:T(8,128)(2,1)S(1)} %bitcast.14), channel_id=1, replica_groups=mesh['x'=4,'y'=4,'z'=8,'core'=2] {'x'}, dimensions={0} | all-to-all | bytes 8388608 | tf_op jit(solution)/shard_map/all_to_all | solution.py:55
  211.6 4.5 %reduce_sum.73 = bf16[512,1024]{1,0:T(8,128)(2,1)} reduce(bf16[4,512,1024]{2,1,0:T(8,128)(2,1)} %all_to_all.27, bf16[]{:T(256)} %constant.40.clone.1), dimensions={0}, to_apply=%region_4.5 | reduce | flops 1572864 | bytes 5242882 | tf_op jit(solution)/shard_map/reduce_sum | solution.py:56
  216.1 18.4 %all_to_all.28 = bf16[4,128,1024]{2,1,0:T(8,128)(2,1)S(1)} all-to-all(bf16[4,128,1024]{2,1,0:T(8,128)(2,1)} %bitcast.15), channel_id=1, replica_groups=mesh['x'=4,'y'=4,'z'=8,'core'=2] {'y'}, dimensions={0} | all-to-all | bytes 2097152 | tf_op jit(solution)/shard_map/all_to_all | solution.py:55
  234.5 0.9 reduce_sum.74
  235.4 3.4 %all-to-all-start.3 = ((bf16[8,16,1024]{2,1,0:T(8,128)(2,1)}), bf16[8,16,1024]{2,1,0:T(8,128)(2,1)S(1)}, u32[]{:S(2)}, u32[]{:S(2)}) async-start(bf16[8,16,1024]{2,1,0:T(8,128)(2,1)} %bitcast.4), calls=%async_computation.3 | async-start | bytes 524288 | tf_op jit(solution)/shard_map/all_to_all | solution.py:55
  238.9 5.3 %convolution_convert_fusion.1 = bf16[384,1024]{1,0:T(8,128)(2,1)} fusion(bf16[384,2048]{1,0:T(8,128)(2,1)} %copy-done.1, bf16[2048,1024]{1,0:T(8,128)(2,1)} %all-gather.2.cloned.1.call-done), kind=kOutput, calls=%fused_computation.9 | convolution fusion | flops 1611005952 | bytes 6553600 | tf_op jit(solution)/shard_map/dot_general | solution.py:50
  244.2 5.4 %all-to-all-done.3 = bf16[8,16,1024]{2,1,0:T(8,128)(2,1)S(1)} async-done(((bf16[8,16,1024]{2,1,0:T(8,128)(2,1)}), bf16[8,16,1024]{2,1,0:T(8,128)(2,1)S(1)}, u32[]{:S(2)}, u32[]{:S(2)}) %all-to-all-start.3) | async-done | bytes 262176 | tf_op jit(solution)/shard_map/all_to_all | solution.py:55
  249.6 0.6 multiply_bitcast_fusion
  (8 shorter events, 0.1 us)
Async XLA Ops:
  7.2 93.0 %copy-start = (bf16[384,2048]{1,0:T(8,128)(2,1)S(1)}, bf16[384,2048]{1,0:T(8,128)(2,1)}, u32[]{:S(2)}) copy-start(bf16[384,2048]{1,0:T(8,128)(2,1)} %param.13) | copy-start | bytes 4718596
  7.2 87.0 %all-gather.2.cloned.1.call-start = ((), (), s32[]{:S(2)}) async-start(), calls=%async_computation.4 | async-start | bytes 4456448 | tf_op jit(solution)/shard_map/all_gather | solution.py:41
  100.1 14.4 %copy-start.3 = (s32[384]{0:T(512)S(1)}, s32[384]{0:T(512)}, u32[]{:S(2)}) copy-start(s32[384]{0:T(512)} %param.15) | copy-start | bytes 4612
  100.1 46.8 %collective-permute-start = (f32[384,2048]{1,0:T(8,128)}, f32[384,2048]{1,0:T(8,128)}, u32[]{:S(2)}, u32[]{:S(2)}) collective-permute-start(f32[384,2048]{1,0:T(8,128)} %fusion.2), channel_id=1, source_target_pairs={{0,1},{1,0},{2,3},{3,2},{4,5},{5,4},{6,7},{7,6},{8,9},{9,8},{10,11... | collective-permute-start | bytes 9437192 | tf_op jit(solution)/shard_map/ppermute | solution.py:45
  101.5 42.4 %all-to-all-start = ((bf16[128,3,1024]{2,1,0:T(4,128)(2,1)}), bf16[128,3,1024]{2,1,0:T(4,128)(2,1)S(1)}, u32[]{:S(2)}, u32[]{:S(2)}) async-start(bf16[128,3,1024]{2,1,0:T(4,128)(2,1)} %all_to_all.17), calls=%async_computation | async-start | bytes 2097152 | tf_op jit(solution)/shard_map/all_to_all | solution.py:31
  144.5 2.4 copy-start.4
  146.8 4.5 %collective-permute-start.1 = (bf16[384,1024]{1,0:T(8,128)(2,1)S(1)}, bf16[384,1024]{1,0:T(8,128)(2,1)S(1)}, u32[]{:S(2)}, u32[]{:S(2)}) collective-permute-start(bf16[384,1024]{1,0:T(8,128)(2,1)S(1)} %select_select_fusion), channel_id=1, source_target_pairs={{0,1},{1,0},{2,3},{3,2},{4,5},{5,4},{6,7},{7,6},{8,9},{9,8},{10,11... | collective-permute-start | bytes 2359304 | tf_op jit(solution)/shard_map/ppermute | solution.py:34
  150.8 0.7 copy-start.2
  152.5 1.6 copy-start.5
  154.2 2.4 copy-start.1
  235.4 14.1 %all-to-all-start.3 = ((bf16[8,16,1024]{2,1,0:T(8,128)(2,1)}), bf16[8,16,1024]{2,1,0:T(8,128)(2,1)S(1)}, u32[]{:S(2)}, u32[]{:S(2)}) async-start(bf16[8,16,1024]{2,1,0:T(8,128)(2,1)} %bitcast.4), calls=%async_computation.3 | async-start | bytes 524288 | tf_op jit(solution)/shard_map/all_to_all | solution.py:55
Sparse Core Ops, SparseCore 0:
  38.1 55.9 all-gather.1
where the time goes:
time: 258 us; the launch traced here: 257 us
  blocking collectives  104 us (40%)
  waiting for transfers between devices  90.9 us (35%)
  starting transfers between devices  15.9 us (6%)
  between operations  14.9 us (6%)
  matrix products  13.7 us (5%)
  other arithmetic  13.2 us (5%)
  local copies, waits for them, and re-layouts  4.35 us (2%)
    all_to_all x2, blocking collectives, shards(): got = lax.all_to_all(share, axis, split_axis=0, concat_axis=0)  73.4 us
    all_gather x1, waiting for transfers between devices, shards(): weight_t = lax.all_gather(weight_t, ('x', 'y'), axis=0, tiled=True)  56.2 us
    all_gather x1, blocking collectives, shards(): weight_t = lax.all_gather(out_weight.T, 'z', axis=0, tiled=True)  30.8 us
    all_to_all x1, waiting for transfers between devices, shards(): lax.all_to_all(mine, ('x', 'y', 'z'), split_axis=0, concat_axis=0, tiled=...  29.3 us
    all_to_all x1, starting transfers between devices, shards(): lax.all_to_all(mine, ('x', 'y', 'z'), split_axis=0, concat_axis=0, tiled=...  12.3 us
    dot_general x1, matrix products, shards(): lax.dot_general(context, weight_t, (((1,), (1,)), ((), ())), preferred_el...  5.94 us
    reduce_sum x3, other arithmetic, shards(): total = jnp.sum(got.astype(F32), axis=0)  5.44 us
    all_to_all x1, waiting for transfers between devices, shards(): got = lax.all_to_all(share, axis, split_axis=0, concat_axis=0)  5.39 us
  transfers between devices with their start and end apart: 5, of which 3 were waited for; matrix products, arithmetic and copies ran while one was open for 5% of the time, Pallas kernels for 0%

commit v1 on v0

--- a/solution.py
+++ b/solution.py
@@ -37,7 +37,9 @@
         jnp.concatenate([picked, other], axis=1),
         jnp.concatenate([other, picked], axis=1),
     )
-    weight_t = lax.all_gather(out_weight.T, "z", axis=0, tiled=True)
+    weight_t = jnp.concatenate(
+        lax.all_to_all(jnp.stack([out_weight.T] * lax.axis_size("z")), "z", 0, 0), axis=0
+    )
     weight_t = lax.all_gather(weight_t, ("x", "y"), axis=0, tiled=True)
     partial_proj = lax.dot_general(
         context, weight_t, (((1,), (1,)), ((), ())), preferred_element_type=F32

time: 258 us -> 245 us (0.950)
  blocking collectives: 104 us -> 93.7 us
  waiting for transfers between devices: 90.9 us -> 87.8 us
    all_gather x1 -> x0, blocking collectives: 30.8 us -> none  [shards(): weight_t = lax.all_gather(out_weight.T, 'z', axis=0, tiled=True)]
    all_to_all x0 -> x1, blocking collectives: none -> 20.2 us  [shards(): lax.all_to_all(jnp.stack([out_weight.T] * lax.axis_size('z')), 'z', 0, 0)]
    all_gather x1, waiting for transfers between devices: 56.2 us -> 53 us  [shards(): weight_t = lax.all_gather(weight_t, ('x', 'y'), axis=0, tiled=True)]
where the time goes in v1:
time: 245 us; the launch traced here: 244 us
  blocking collectives  93.7 us (38%)
  waiting for transfers between devices  87.8 us (36%)
  starting transfers between devices  15.9 us (6%)
  between operations  14.9 us (6%)
  matrix products  13.7 us (6%)
  other arithmetic  13.2 us (5%)
  local copies, waits for them, and re-layouts  5.24 us (2%)
    all_to_all x2, blocking collectives, shards(): got = lax.all_to_all(share, axis, split_axis=0, concat_axis=0)  73.4 us
    all_gather x1, waiting for transfers between devices, shards(): weight_t = lax.all_gather(weight_t, ('x', 'y'), axis=0, tiled=True)  53 us
    all_to_all x1, waiting for transfers between devices, shards(): lax.all_to_all(mine, ('x', 'y', 'z'), split_axis=0, concat_axis=0, tiled=...  29.3 us
    all_to_all x1, blocking collectives, shards(): lax.all_to_all(jnp.stack([out_weight.T] * lax.axis_size('z')), 'z', 0, 0)  20.2 us
    all_to_all x1, starting transfers between devices, shards(): lax.all_to_all(mine, ('x', 'y', 'z'), split_axis=0, concat_axis=0, tiled=...  12.3 us
    dot_general x1, matrix products, shards(): lax.dot_general(context, weight_t, (((1,), (1,)), ((), ())), preferred_el...  5.94 us
    reduce_sum x3, other arithmetic, shards(): total = jnp.sum(got.astype(F32), axis=0)  5.44 us
    all_to_all x1, waiting for transfers between devices, shards(): got = lax.all_to_all(share, axis, split_axis=0, concat_axis=0)  5.39 us
  transfers between devices with their start and end apart: 5, of which 3 were waited for; matrix products, arithmetic and copies ran while one was open for 5% of the time, Pallas kernels for 0%

profile of v1, /device:TPU:2, one launch (start us, length us, event | category | flops | bytes accessed | tf_op | source)
XLA Modules:
  0.0 244.4 jit_solution(16088305914626195969)
XLA Ops:
  7.2 0.0 copy-start
  7.2 0.0 all-gather.2.cloned.1.call-start
  7.2 0.9 stack.2
  8.1 20.2 %all_to_all.32 = bf16[8,16,1024]{2,1,0:T(8,128)(2,1)} all-to-all(bf16[8,16,1024]{2,1,0:T(8,128)(2,1)S(1)} %stack.2), channel_id=1, replica_groups=mesh['x'=4,'y'=4,'z'=8,'core'=2] {'z'}, dimensions={0} | all-to-all | bytes 524288 | tf_op jit(solution)/shard_map/all_to_all | solution.py:41
  28.4 0.0 all-gather.2.cloned.1.call-update
  28.4 53.0 %all-gather.2.cloned.1.call-done = bf16[2048,1024]{1,0:T(8,128)(2,1)} async-done(((bf16[128,1024]{1,0:T(8,128)(2,1)}), bf16[2048,1024]{1,0:T(8,128)(2,1)}) %all-gather.2.cloned.1.call-update) | async-done | bytes 4194320 | tf_op jit(solution)/shard_map/all_gather | solution.py:43
  81.4 5.9 %fusion.2 = f32[384,2048]{1,0:T(8,128)} fusion(bf16[384,1024]{1,0:T(8,128)(2,1)} %param.8, bf16[2048,1024]{1,0:T(8,128)(2,1)} %all-gather.2.cloned.1.call-done), kind=kOutput, calls=%fused_computation.23 | convolution fusion | flops 1610612736 | bytes 8126464 | tf_op jit(solution)/shard_map/dot_general | solution.py:44
  87.3 0.0 copy-start.3
  87.4 0.0 collective-permute-start
  87.4 0.0 copy-done
  87.4 0.1 constant_dynamic-slice_fusion
  87.4 1.3 all_to_all.21
  88.7 12.3 %all-to-all-start.1 = ((bf16[128,3,1024]{2,1,0:T(4,128)(2,1)}), bf16[128,3,1024]{2,1,0:T(4,128)(2,1)S(1)}, u32[]{:S(2)}, u32[]{:S(2)}) async-start(bf16[128,3,1024]{2,1,0:T(4,128)(2,1)} %all_to_all.21), calls=%async_computation.1 | async-start | bytes 2097152 | tf_op jit(solution)/shard_map/all_to_all | solution.py:31
  101.7 0.0 copy-done.3
  101.8 29.3 %all-to-all-done.1 = bf16[128,3,1024]{2,1,0:T(4,128)(2,1)S(1)} async-done(((bf16[128,3,1024]{2,1,0:T(4,128)(2,1)}), bf16[128,3,1024]{2,1,0:T(4,128)(2,1)S(1)}, u32[]{:S(2)}, u32[]{:S(2)}) %all-to-all-start.1) | async-done | bytes 786464 | tf_op jit(solution)/shard_map/all_to_all | solution.py:31
  131.1 0.7 all_to_all.23
  131.8 0.0 copy-start.4
  131.8 2.1 gather_fusion
  133.9 0.2 select_select_fusion
  134.1 0.1 collective-permute-start.1
  134.2 0.0 collective-permute-done
  134.2 0.0 copy-done.4
  134.2 3.9 %fusion.1 = (f32[384]{0:T(512)S(1)}, f32[384,2048]{1,0:T(8,128)S(1)}) fusion(f32[2048]{0:T(1024)S(1)} %copy-done.4, f32[384,2048]{1,0:T(8,128)} %fusion.2, f32[384,2048]{1,0:T(8,128)} %collective-permute-done, bf16[384,2048]{1,0:T(8,128)(2,1)} %param.9), kind=kLoop, calls=%fused_computation.22 | loop fusion | flops 3931776 | bytes 11019776 | tf_op jit(solution)/shard_map/reduce_sum | solution.py:12
  138.0 0.0 copy-start.2
  138.1 0.5 multiply_reduce_fusion.1
  138.5 0.0 collective-permute-done.1
  138.5 0.2 copy-done.2
  138.7 1.0 fusion
  139.8 0.0 copy-start.5
  139.8 1.6 multiply_convert_fusion
  141.4 0.0 copy-done.5
  141.4 0.0 copy-start.1
  141.4 2.4 convolution_convert_fusion
  143.8 0.0 copy-done.1
  143.8 55.0 %all_to_all.33 = bf16[4,512,1024]{2,1,0:T(8,128)(2,1)} all-to-all(bf16[4,512,1024]{2,1,0:T(8,128)(2,1)S(1)} %bitcast.15), channel_id=1, replica_groups=mesh['x'=4,'y'=4,'z'=8,'core'=2] {'x'}, dimensions={0} | all-to-all | bytes 8388608 | tf_op jit(solution)/shard_map/all_to_all | solution.py:57
  198.9 4.5 %reduce_sum.73 = bf16[512,1024]{1,0:T(8,128)(2,1)} reduce(bf16[4,512,1024]{2,1,0:T(8,128)(2,1)} %all_to_all.33, bf16[]{:T(256)} %constant.40.clone.1), dimensions={0}, to_apply=%region_4.5 | reduce | flops 1572864 | bytes 5242882 | tf_op jit(solution)/shard_map/reduce_sum | solution.py:58
  203.3 18.4 %all_to_all.34 = bf16[4,128,1024]{2,1,0:T(8,128)(2,1)S(1)} all-to-all(bf16[4,128,1024]{2,1,0:T(8,128)(2,1)} %bitcast.16), channel_id=1, replica_groups=mesh['x'=4,'y'=4,'z'=8,'core'=2] {'y'}, dimensions={0} | all-to-all | bytes 2097152 | tf_op jit(solution)/shard_map/all_to_all | solution.py:57
  221.8 0.9 reduce_sum.74
  222.7 3.4 %all-to-all-start.4 = ((bf16[8,16,1024]{2,1,0:T(8,128)(2,1)}), bf16[8,16,1024]{2,1,0:T(8,128)(2,1)S(1)}, u32[]{:S(2)}, u32[]{:S(2)}) async-start(bf16[8,16,1024]{2,1,0:T(8,128)(2,1)} %bitcast.5), calls=%async_computation.4 | async-start | bytes 524288 | tf_op jit(solution)/shard_map/all_to_all | solution.py:57
  226.1 5.3 %convolution_convert_fusion.1 = bf16[384,1024]{1,0:T(8,128)(2,1)} fusion(bf16[384,2048]{1,0:T(8,128)(2,1)} %copy-done.1, bf16[2048,1024]{1,0:T(8,128)(2,1)} %all-gather.2.cloned.1.call-done), kind=kOutput, calls=%fused_computation.9 | convolution fusion | flops 1611005952 | bytes 6553600 | tf_op jit(solution)/shard_map/dot_general | solution.py:52
  231.4 5.4 %all-to-all-done.4 = bf16[8,16,1024]{2,1,0:T(8,128)(2,1)S(1)} async-done(((bf16[8,16,1024]{2,1,0:T(8,128)(2,1)}), bf16[8,16,1024]{2,1,0:T(8,128)(2,1)S(1)}, u32[]{:S(2)}, u32[]{:S(2)}) %all-to-all-start.4) | async-done | bytes 262176 | tf_op jit(solution)/shard_map/all_to_all | solution.py:57
  236.9 0.6 multiply_bitcast_fusion
  (8 shorter events, 0.1 us)
Async XLA Ops:
  7.2 80.2 %copy-start = (bf16[384,2048]{1,0:T(8,128)(2,1)S(1)}, bf16[384,2048]{1,0:T(8,128)(2,1)}, u32[]{:S(2)}) copy-start(bf16[384,2048]{1,0:T(8,128)(2,1)} %param.13) | copy-start | bytes 4718596
  7.2 74.2 %all-gather.2.cloned.1.call-start = ((), (), s32[]{:S(2)}) async-start(), calls=%async_computation.5 | async-start | bytes 4456448 | tf_op jit(solution)/shard_map/all_gather | solution.py:43
  87.3 14.4 %copy-start.3 = (s32[384]{0:T(512)S(1)}, s32[384]{0:T(512)}, u32[]{:S(2)}) copy-start(s32[384]{0:T(512)} %param.15) | copy-start | bytes 4612
  87.4 46.8 %collective-permute-start = (f32[384,2048]{1,0:T(8,128)}, f32[384,2048]{1,0:T(8,128)}, u32[]{:S(2)}, u32[]{:S(2)}) collective-permute-start(f32[384,2048]{1,0:T(8,128)} %fusion.2), channel_id=1, source_target_pairs={{0,1},{1,0},{2,3},{3,2},{4,5},{5,4},{6,7},{7,6},{8,9},{9,8},{10,11... | collective-permute-start | bytes 9437192 | tf_op jit(solution)/shard_map/ppermute | solution.py:47
  88.7 42.4 %all-to-all-start.1 = ((bf16[128,3,1024]{2,1,0:T(4,128)(2,1)}), bf16[128,3,1024]{2,1,0:T(4,128)(2,1)S(1)}, u32[]{:S(2)}, u32[]{:S(2)}) async-start(bf16[128,3,1024]{2,1,0:T(4,128)(2,1)} %all_to_all.21), calls=%async_computation.1 | async-start | bytes 2097152 | tf_op jit(solution)/shard_map/all_to_all | solution.py:31
  131.8 2.4 copy-start.4
  134.1 4.5 %collective-permute-start.1 = (bf16[384,1024]{1,0:T(8,128)(2,1)S(1)}, bf16[384,1024]{1,0:T(8,128)(2,1)S(1)}, u32[]{:S(2)}, u32[]{:S(2)}) collective-permute-start(bf16[384,1024]{1,0:T(8,128)(2,1)S(1)} %select_select_fusion), channel_id=1, source_target_pairs={{0,1},{1,0},{2,3},{3,2},{4,5},{5,4},{6,7},{7,6},{8,9},{9,8},{10,11... | collective-permute-start | bytes 2359304 | tf_op jit(solution)/shard_map/ppermute | solution.py:34
  138.0 0.7 copy-start.2
  139.8 1.6 copy-start.5
  141.4 2.4 copy-start.1
  222.7 14.1 %all-to-all-start.4 = ((bf16[8,16,1024]{2,1,0:T(8,128)(2,1)}), bf16[8,16,1024]{2,1,0:T(8,128)(2,1)S(1)}, u32[]{:S(2)}, u32[]{:S(2)}) async-start(bf16[8,16,1024]{2,1,0:T(8,128)(2,1)} %bitcast.5), calls=%async_computation.4 | async-start | bytes 524288 | tf_op jit(solution)/shard_map/all_to_all | solution.py:57
Sparse Core Ops, SparseCore 0:
  28.5 52.8 all-gather.1
